TPU v7x, 256 devices: a whole 4x4x8 slice. The times are simulated.
256 devices in a mesh: px: 32 (over z, x), py: 8 (over y, core).
Axes of the slice: x: 4, y: 4, z: 8, core: 2. Of those that a mesh axis runs over, the one named last changes fastest.
Arguments:
- counts: int32 [32], replicated, may hold values from 1 to 6, 64 in all
- coefficient: float32 [192, 8, 4096], P('px', 'py'), may hold values from 0.2 to 5
- signs: int32 [192, 8, 4096], P('px', 'py'), may hold values from 0 to 1
- basis_old: float32 [192, 8, 16, 4096], P('px', 'py'), may hold values from -8 to 8
- basis_last: float32 [192, 8, 16, 4096], P('px', 'py'), may hold values from -8 to 8
- residual_factor: float32 [16, 16], replicated, may hold values from -12 to 12
- previous_coef: float32 [32, 16], replicated, may hold values from -12 to 12
- sample_rows: int32 [2048], replicated, may hold values from 0 to 2097151, as said below
Outputs:
- new_block: float32 [192, 8, 16, 4096], P('px', 'py')
- sketch: float32 [48, 2048], P(None, ('px', 'py'))
- solution: float32 [32, 16], replicated
Inputs may be any that keep to these rules, and one draw needn't show every extreme that they name: Index i of px owns counts[i] consecutive patch columns, in px order; the largest count is exactly 6. `sample_rows`: distinct cell numbers, among them 0 and 2097151.
All inputs are finite; a program needn't handle non-finite values.
Results may differ from a plain program's by a relative error of at most 0.0003.
Values sent between devices are 32-bit elements; how exact they have to be, the bound alone decides.
No kernel may reach another device: no remote copies, remote signals or barrier semaphores. Data moves between devices by JAX's collectives and lax.ppermute only.
A program may use at most 256 MiB of HBM per device.

v0:
```python
import math
import jax
import jax.numpy as jnp
from jax import lax
from jax.sharding import PartitionSpec as P

PS = 16
K = 2048
MEANX = 2
CAP = 6
CELLS = 4096
highest = lax.Precision.HIGHEST


def extended(block, sides, width):
    for axis, dim in sides:
        count = lax.axis_size(axis)
        forward = [(i, i + 1) for i in range(count - 1)]
        backward = [(target, source) for source, target in forward]
        low = lax.ppermute(
            lax.slice_in_dim(block, block.shape[dim] - width, None, axis=dim), axis, forward
        )
        high = lax.ppermute(lax.slice_in_dim(block, 0, width, axis=dim), axis, backward)
        block = jnp.concatenate([low, block, high], axis=dim)
    return block


def parity_of(values):
    folded = values
    for amount in (16, 8, 4, 2, 1):
        folded = jnp.bitwise_xor(folded, jnp.right_shift(folded, amount))
    return jnp.bitwise_and(folded, 1)


def sign_table(length):
    indices = jnp.arange(length, dtype=jnp.int32)
    parity = parity_of(jnp.bitwise_and(indices[:, None], indices[None, :]))
    return (1 - 2 * parity).astype(jnp.float32)


def transform_cells(values):
    inner_len = min(CELLS, 128)
    outer_len = CELLS // inner_len
    shaped = values.reshape(values.shape[:-1] + (outer_len, inner_len))
    shaped = jnp.einsum("sjab,bd->sjad", shaped, sign_table(inner_len), precision=highest)
    shaped = jnp.einsum("ca,sjad->sjcd", sign_table(outer_len), shaped, precision=highest)
    return shaped.reshape(values.shape)


def shift_pair(cube_vals, low_plane, high_plane, axis_pos):
    below = jnp.concatenate(
        [
            jnp.expand_dims(low_plane, axis_pos),
            lax.slice_in_dim(cube_vals, 0, PS - 1, axis=axis_pos),
        ],
        axis=axis_pos,
    )
    above = jnp.concatenate(
        [lax.slice_in_dim(cube_vals, 1, PS, axis=axis_pos), jnp.expand_dims(high_plane, axis_pos)],
        axis=axis_pos,
    )
    return (below, above)


def apply_operator(last_local, kappa_local, held_count, slot_ids):
    channels = last_local.shape[1] + 1
    plane_size = PS * PS
    joined = jnp.concatenate([last_local, kappa_local[:, None]], axis=1)
    cube_vals = joined.reshape(CAP, channels, PS, PS, PS)
    first_face = cube_vals[0, :, 0].reshape(channels, plane_size)
    last_slot = lax.dynamic_index_in_dim(cube_vals, held_count - 1, 0, keepdims=False)
    last_face = last_slot[:, PS - 1].reshape(channels, plane_size)
    x_ghost = extended(jnp.stack([first_face, last_face]), (("px", 0),), 1)
    y_planes = jnp.stack([cube_vals[:, :, :, 0], cube_vals[:, :, :, PS - 1]]).reshape(
        2, CAP, channels, plane_size
    )
    y_ghost = extended(y_planes, (("py", 0),), 1)
    ghost_low = x_ghost[0].reshape(channels, PS, PS)
    ghost_high = x_ghost[3].reshape(channels, PS, PS)
    x_low = jnp.concatenate([ghost_low[None], cube_vals[:-1, :, PS - 1]], axis=0)
    next_faces = jnp.concatenate([cube_vals[1:, :, 0], jnp.zeros_like(cube_vals[:1, :, 0])], axis=0)
    x_high = jnp.where(
        (slot_ids == held_count - 1)[:, None, None, None], ghost_high[None], next_faces
    )
    y_low = y_ghost[0].reshape(CAP, channels, PS, PS)
    y_high = y_ghost[3].reshape(CAP, channels, PS, PS)
    z_zero = jnp.zeros((CAP, channels, PS, PS), jnp.float32)
    centre_vals = cube_vals[:, :-1]
    centre_kappa = cube_vals[:, -1:]
    diag_sum = jnp.zeros_like(centre_kappa)
    weighted = jnp.zeros_like(centre_vals)
    for low_plane, high_plane, axis_pos in (
        (x_low, x_high, 2),
        (y_low, y_high, 3),
        (z_zero, z_zero, 4),
    ):
        kappa_pair = shift_pair(centre_kappa, low_plane[:, -1:], high_plane[:, -1:], axis_pos)
        value_pair = shift_pair(centre_vals, low_plane[:, :-1], high_plane[:, :-1], axis_pos)
        for near_kappa, near_vals in zip(kappa_pair, value_pair):
            weight = 0.5 * (centre_kappa + near_kappa)
            diag_sum = diag_sum + weight
            weighted = weighted + weight * near_vals
    summed = diag_sum * centre_vals - weighted
    return summed.reshape(CAP, channels - 1, CELLS)


def normal_parts(sketch_cols, proj_coef, previous_coef, residual_factor):
    pair_count = proj_coef.shape[0]
    width_rhs = proj_coef.shape[1]
    pair_rows = sketch_cols[:pair_count]
    first_image = jnp.einsum("ab,ak->bk", previous_coef, pair_rows, precision=highest)
    second_image = (
        jnp.einsum("ab,ak->bk", proj_coef, pair_rows, precision=highest) + sketch_cols[pair_count:]
    )
    images = jnp.concatenate([first_image, second_image], axis=0)
    target = jnp.einsum("ab,ak->bk", residual_factor, sketch_cols[:width_rhs], precision=highest)
    return (
        jnp.dot(images, images.T, precision=highest),
        jnp.dot(images, target.T, precision=highest),
    )


def solve_normal(normal_gram, normal_cross):
    factor_low = jnp.linalg.cholesky(normal_gram)
    middle = lax.linalg.triangular_solve(factor_low, normal_cross, left_side=True, lower=True)
    return lax.linalg.triangular_solve(
        factor_low, middle, left_side=True, lower=True, transpose_a=True
    )


def body(
    counts, coefficient, signs, basis_old, basis_last, residual_factor, previous_coef, sample_rows
):
    px_index = lax.axis_index("px")
    py_index = lax.axis_index("py")
    py_count = lax.axis_size("py")
    device_count = lax.axis_size("px") * py_count
    total_cells = MEANX * device_count * CELLS
    offsets = jnp.cumsum(counts) - counts
    held_count = counts[px_index]
    slot_ids = jnp.arange(CAP, dtype=jnp.int32)
    live_weight = (slot_ids < held_count).astype(jnp.float32)
    old_local = basis_old[:, 0] * live_weight[:, None, None]
    last_local = basis_last[:, 0] * live_weight[:, None, None]
    image = (
        apply_operator(last_local, coefficient[:, 0], held_count, slot_ids)
        * live_weight[:, None, None]
    )
    pair = jnp.concatenate([old_local, last_local], axis=1)
    local_gram = jnp.einsum("sac,sbc->ab", pair, image, precision=highest)
    patch_ids = (offsets[px_index] + slot_ids) * py_count + py_index
    sign_flips = (1 - 2 * signs[:, 0]).astype(jnp.float32)
    share_width = K // device_count
    share_start = (px_index * py_count + py_index) * share_width
    proj_coef = lax.psum(local_gram, ("px", "py")) / total_cells
    new_local = image - jnp.einsum("sac,ab->sbc", pair, proj_coef, precision=highest)
    spread = transform_cells(jnp.concatenate([pair, new_local], axis=1) * sign_flips[:, None, :])
    picked = jnp.take(spread, sample_rows % CELLS, axis=2)
    parity = parity_of(jnp.bitwise_and(patch_ids[:, None], (sample_rows // CELLS)[None, :]))
    weights = (1 - 2 * parity).astype(jnp.float32) * live_weight[:, None]
    partial_value = jnp.einsum("sk,sjk->jk", weights, picked, precision=highest) * (
        1.0 / math.sqrt(total_cells)
    )
    sketch_whole = lax.psum(partial_value, ("px", "py"))
    sketch_mine = lax.dynamic_slice_in_dim(sketch_whole, share_start, share_width, 1)
    normal_gram, normal_cross = normal_parts(
        sketch_whole, proj_coef, previous_coef, residual_factor
    )
    solution = solve_normal(normal_gram, normal_cross)
    return (new_local[:, None], sketch_mine, solution)


def solution(mesh):
    in_specs = (
        P(),
        P("px", "py", None),
        P("px", "py", None),
        P("px", "py", None, None),
        P("px", "py", None, None),
        P(),
        P(),
        P(),
    )
    out_specs = (P("px", "py", None, None), P(None, ("px", "py")), P())
    return jax.shard_map(body, mesh=mesh, in_specs=in_specs, out_specs=out_specs, check_vma=False)
```

profile of v0, /device:TPU:1, one launch (start us, length us, event | category | flops | bytes accessed | tf_op | source)
XLA Modules:
  0.0 603.8 jit_solution(3196232569332509484)
XLA Ops:
  7.2 1.2 dynamic_slice.13
  9.1 2.3 bitcast_multiply_fusion.2
  11.7 2.4 copy.21
  14.0 8.6 %reshape.92 = f32[6,17,16,16,16]{4,3,2,0,1:T(8,128)} reshape(f32[6,17,4096]{2,0,1:T(8,128)} %copy.21) | data formatting | bytes 3342336 | tf_op jit(solution)/shard_map/reshape | solution.py:69
  22.6 0.9 slice.167
  23.7 1.3 collective-permute-start.1
  26.3 3.2 constant_dynamic-slice_fusion.1
  29.5 3.9 copy.22
  33.3 0.9 slice.163
  34.3 5.2 collective-permute-start
  39.5 10.8 %slice_reduce_fusion = (f32[6,17,16,16]{3,2,0,1:T(8,128)}, f32[6,17,16,16]{3,2,0,1:T(8,128)}) fusion(f32[6,17,16,16,16]{4,3,2,0,1:T(8,128)} %reshape.92), kind=kLoop, calls=%fused_computation.34 | loop fusion | bytes 417792 | tf_op jit(solution)/shard_map/slice | solution.py:74
  50.2 1.5 reshape.112
  51.7 0.8 copy.47
  52.5 4.6 collective-permute-start.2
  57.1 1.5 reshape.113
  58.6 0.8 copy.48
  59.3 3.0 collective-permute-start.3
  62.4 17.5 %fusion.102 = (f32[6,16,15,16,16]{4,3,2,0,1:T(8,128)}, f32[6,16,15,16,16]{4,3,2,0,1:T(8,128)}) fusion(f32[6,17,16,16,16]{4,3,2,0,1:T(8,128)} %reshape.92), kind=kLoop, calls=%fused_computation.173 | loop fusion | bytes 5898240 | tf_op jit(solution)/shard_map/slice | solution.py:59
  79.8 1.2 slice_bitcast_fusion.1
  81.1 9.2 %fusion.101 = (f32[6,16,16,15,16]{4,3,2,0,1:T(8,128)}, f32[6,16,16,15,16]{4,3,2,0,1:T(8,128)}) fusion(f32[6,17,16,16,16]{4,3,2,0,1:T(8,128)S(1)} %bitcast.139), kind=kLoop, calls=%fused_computation.172 | loop fusion | bytes 5898240 | tf_op jit(solution)/shard_map/slice | solution.py:59
  90.3 9.8 %fusion.100 = (f32[6,16,16,16,15]{4,3,2,0,1:T(8,128)}, f32[6,16,16,16,15]{4,3,2,0,1:T(8,128)}) fusion(f32[6,17,16,16,16]{4,3,2,0,1:T(8,128)S(1)} %bitcast.139), kind=kLoop, calls=%fused_computation.171 | loop fusion | bytes 5898240 | tf_op jit(solution)/shard_map/slice | solution.py:54
  100.1 1.4 fusion.99
  101.5 1.2 fusion.97
  102.8 1.3 fusion.98
  105.3 1.4 copy.54
  106.7 1.4 copy.55
  109.1 4.0 bitcast_multiply_fusion.1
  114.3 1.3 copy.53
  115.8 0.8 reduce.7
  116.7 1.3 pad_select_fusion
  118.1 0.8 slice_bitcast_fusion.3
  118.9 3.5 fusion.30
  122.4 1.3 slice_bitcast_fusion
  123.7 0.9 copy.31
  124.6 1.2 reshape_squeeze.7
  125.8 2.1 slice.185
  127.9 1.4 slice.175
  129.3 0.9 copy.29
  130.2 1.2 reshape_squeeze.6
  131.4 2.1 slice.182
  133.5 0.8 slice.171
  134.3 5.0 add_bitcast_fusion
  139.3 37.8 %fusion = f32[6,16,16,16,16]{4,3,2,0,1:T(8,128)} fusion(f32[6,17,16,16,16]{4,3,2,0,1:T(8,128)} %reshape.92, f32[6,16,15,16,16]{4,3,2,0,1:T(8,128)} %get-tuple-element.29, f32[6,16,1,16,16]{4,3,2,0,1:T(8,128)} %get-tuple-element.41, f32[6,16,1,16,16]{4,3,2,0,1:T(8,128)} %get-tuple-element.40, f32[6,16,15,16,16]{4,3,2,0,1:T(8,128)} %get-tuple-element.28, ...), kind=kLoop, calls=%fused_computation.2 | loop fusion | flops 6684672 | bytes 13074432 | tf_op jit(solution)/shard_map/sub | solution.py:103
  177.1 10.5 %reshape.114 = f32[6,16,4096]{2,0,1:T(8,128)} reshape(f32[6,16,16,16,16]{4,3,2,0,1:T(8,128)} %fusion) | data formatting | bytes 3145728 | tf_op jit(solution)/shard_map/reshape | solution.py:104
  187.6 4.7 fusion.14
  192.3 80.0 %psum.14 = f32[32,16]{0,1:T(8,128)S(1)} all-reduce(f32[32,16]{0,1:T(8,128)S(1)} %fusion.14), channel_id=1, replica_groups=mesh['px'=32,'py'=8] {'px','py'}, use_global_device_ids=true, to_apply=%region_0.0 | all-reduce | flops 512 | bytes 4096 | tf_op jit(solution)/shard_map/psum | solution.py:155
  272.4 4.1 fusion.6
  276.8 0.9 copy-done.5
  277.6 4.0 fusion.7
  281.6 5.7 convolution_bitcast_fusion.1
  287.3 9.7 %copy.50 = f32[6,48,32,128]{1,0,3,2:T(8,128)} copy(f32[6,48,32,128]{3,2,1,0:T(8,128)} %convolution_bitcast_fusion.1) | data formatting | bytes 9437184 | tf_op jit(solution)/shard_map/reshape | solution.py:47
  297.0 21.6 %gather_fusion = f32[2048,6,48]{2,1,0:T(8,128)} fusion(f32[6,48,4096]{1,0,2:T(8,128)} %bitcast.140, s32[2048]{0:T(1024)S(1)} %copy-done.10), kind=kCustom, calls=%fused_computation | custom fusion | bytes 4726784 | tf_op jit(solution)/shard_map/jit(_take)/gather | solution.py:158
  318.6 13.2 %multiply_reduce_fusion = f32[2048,48]{1,0:T(8,128)S(1)} fusion(f32[2048,6,48]{2,1,0:T(8,128)} %gather_fusion, f32[2048,6]{1,0:T(8,128)S(1)} %copy-done.7, pred[2048]{0:T(1024)(128)(4,1)S(1)} %copy-done.15), kind=kLoop, calls=%fused_computation.12 | loop fusion | flops 1671168 | bytes 2803712
  332.2 0.8 multiply_bitcast_fusion
  333.0 248.0 %all-reduce.7.cloned.1.call-done = f32[48,2048]{1,0:T(8,128)} async-done(((f32[48,2048]{1,0:T(8,128)}), f32[48,2048]{1,0:T(8,128)}) %all-reduce.7.cloned.1.call-update) | async-done | bytes 393232 | tf_op jit(solution)/shard_map/psum | solution.py:164
  581.0 0.8 constant_dynamic-slice_fusion
  581.8 0.7 copy.37
  582.5 1.2 convolution_add_fusion
  583.7 1.2 convolution_bitcast_fusion.2
  585.3 2.7 fusion.27
  588.1 0.7 fusion.23
  588.8 2.9 cholesky.16
  593.0 2.4 custom-call.8
  595.7 0.8 fusion.60
  (75 shorter events, 7.4 us)
Async XLA Ops:
  7.2 576.6 %copy-start = (f32[32,16]{0,1:T(8,128)S(1)}, f32[32,16]{0,1:T(8,128)}, u32[]{:S(2)}) copy-start(f32[32,16]{0,1:T(8,128)} %param.14) | copy-start | bytes 6148
  7.2 4.3 copy-start.9
  7.2 573.8 %all-reduce.7.cloned.1.call-start = ((), (), s32[]{:S(2)}) async-start(), calls=%async_computation | async-start | bytes 786432 | tf_op jit(solution)/shard_map/psum | solution.py:164
  9.1 104.6 %copy-start.12 = (f32[6]{0:T(128)}, f32[6]{0:T(128)S(1)}, u32[]{:S(2)}) copy-start(f32[6]{0:T(128)S(1)} %compare_convert_fusion) | copy-start | bytes 76
  23.7 92.0 %collective-permute-start.1 = (f32[1,17,256]{2,0,1:T(1,128)S(1)}, f32[1,17,256]{2,0,1:T(1,128)S(1)}, u32[]{:S(2)}, u32[]{:S(2)}) collective-permute-start(f32[1,17,256]{2,0,1:T(1,128)S(1)} %stack_reshape_squeeze.7), channel_id=1, source_target_pairs={{8,0},{16,8},{24,16},{32,24},{40,32},{48,40},{56,48},{64,56},{72,6... | collective-permute-start | bytes 52232 | tf_op jit(solution)/shard_map/ppermute | solution.py:23
  34.3 81.5 %collective-permute-start = (f32[1,17,256]{2,0,1:T(1,128)S(1)}, f32[1,17,256]{2,0,1:T(1,128)}, u32[]{:S(2)}, u32[]{:S(2)}) collective-permute-start(f32[1,17,256]{2,0,1:T(1,128)S(1)} %copy.46), channel_id=1, source_target_pairs={{0,8},{8,16},{16,24},{24,32},{32,40},{40,48},{48,56},{56,64},{64,7... | collective-permute-start | bytes 52232 | tf_op jit(solution)/shard_map/ppermute | solution.py:20
  52.5 76.8 %collective-permute-start.2 = (f32[1,6,17,256]{3,0,2,1:T(1,128)}, f32[1,6,17,256]{3,0,2,1:T(1,128)}, u32[]{:S(2)}, u32[]{:S(2)}) collective-permute-start(f32[1,6,17,256]{3,0,2,1:T(1,128)} %copy.47), channel_id=1, source_target_pairs={{0,1},{1,2},{2,3},{3,4},{4,5},{5,6},{6,7},{8,9},{9,10},{10,11},{11... | collective-permute-start | bytes 313352 | tf_op jit(solution)/shard_map/ppermute | solution.py:20
  58.6 21.2 %slice-start = ((s8[13369344]{0:T(1024)(128)(4,1)}), s8[4194304]{0:T(1024)(128)(4,1)S(1)}, s32[]{:S(2)}) async-start(s8[13369344]{0:T(1024)(128)(4,1)} %bitcast.138), calls=%async_computation.1 | async-start | bytes 8388608
  59.3 20.5 %slice-start.1 = ((s8[13369344]{0:T(1024)(128)(4,1)}), s8[4194304]{0:T(1024)(128)(4,1)S(1)}, s32[]{:S(2)}) async-start(s8[13369344]{0:T(1024)(128)(4,1)} %bitcast.138), calls=%async_computation.2 | async-start | bytes 8388608
  59.3 20.5 %slice-start.2 = ((s8[13369344]{0:T(1024)(128)(4,1)}), s8[4194304]{0:T(1024)(128)(4,1)S(1)}, s32[]{:S(2)}) async-start(s8[13369344]{0:T(1024)(128)(4,1)} %bitcast.138), calls=%async_computation.3 | async-start | bytes 8388608
  59.3 20.5 %slice-start.3 = ((s8[13369344]{0:T(1024)(128)(4,1)}), s8[786432]{0:T(1024)(128)(4,1)S(1)}, s32[]{:S(2)}) async-start(s8[13369344]{0:T(1024)(128)(4,1)} %bitcast.138), calls=%async_computation.4 | async-start | bytes 1572864
  59.3 64.3 %collective-permute-start.3 = (f32[1,6,17,256]{3,0,2,1:T(1,128)}, f32[1,6,17,256]{3,0,2,1:T(1,128)}, u32[]{:S(2)}, u32[]{:S(2)}) collective-permute-start(f32[1,6,17,256]{3,0,2,1:T(1,128)} %copy.48), channel_id=1, source_target_pairs={{1,0},{2,1},{3,2},{4,3},{5,4},{6,5},{7,6},{9,8},{10,9},{11,10},{12... | collective-permute-start | bytes 313352 | tf_op jit(solution)/shard_map/ppermute | solution.py:23
  100.1 3.9 copy-start.11
  100.1 5.1 copy-start.3
  101.5 5.2 copy-start.4
  102.8 5.4 copy-start.8
  102.8 5.5 copy-start.16
  116.7 5.6 copy-start.6
  177.1 10.5 %copy-start.13 = (f32[6]{0:T(128)S(1)}, f32[6]{0:T(128)}, u32[]{:S(2)}) copy-start(f32[6]{0:T(128)} %copy-done.12) | copy-start | bytes 76
  272.3 5.3 copy-start.1
  272.3 5.3 copy-start.2
  276.5 1.1 copy-start.5
  287.3 9.7 %copy-start.10 = (s32[2048]{0:T(1024)S(1)}, s32[2048]{0:T(1024)}, u32[]{:S(2)}) copy-start(s32[2048]{0:T(1024)} %get-tuple-element.33) | copy-start | bytes 24580
  297.0 21.6 %copy-start.7 = (f32[2048,6]{1,0:T(8,128)S(1)}, f32[2048,6]{1,0:T(8,128)}, u32[]{:S(2)}) copy-start(f32[2048,6]{1,0:T(8,128)} %copy.53) | copy-start | bytes 147460
  297.0 21.6 %copy-start.15 = (pred[2048]{0:T(1024)(128)(4,1)S(1)}, pred[2048]{0:T(1024)(128)(4,1)}, u32[]{:S(2)}) copy-start(pred[2048]{0:T(1024)(128)(4,1)} %compare_and_fusion) | copy-start | bytes 6148
  318.6 266.7 %copy-start.14 = (f32[16,16]{1,0:T(8,128)S(1)}, f32[16,16]{1,0:T(8,128)}, u32[]{:S(2)}) copy-start(f32[16,16]{1,0:T(8,128)} %param.13) | copy-start | bytes 3076
Sparse Core Ops, SparseCore 0:
  333.1 247.8 all-reduce.6
where the time goes:
time: 612 us; the launch traced here: 604 us
  waiting for transfers between devices  248 us (41%)
  local copies, waits for them, and re-layouts  139 us (23%)
  other arithmetic  81.1 us (13%)
  blocking collectives  80 us (13%)
  matrix products  25.8 us (4%)
  between operations  16.2 us (3%)
  starting transfers between devices  14.1 us (2%)
    psum x1, waiting for transfers between devices, body(): sketch_whole = lax.psum(partial_value, ('px', 'py'))  248 us
    psum x1, blocking collectives, body(): proj_coef = lax.psum(local_gram, ('px', 'py')) / total_cells  80 us
    sub x1, other arithmetic, apply_operator(): summed = diag_sum * centre_vals - weighted  37.8 us
    slice x2, local copies, waits for them, and re-layouts, shift_pair(): lax.slice_in_dim(cube_vals, 1, PS, axis=axis_pos)  26.7 us
    gather x1, local copies, waits for them, and re-layouts, body(): picked = jnp.take(spread, sample_rows % CELLS, axis=2)  21.6 us
    slice x4, local copies, waits for them, and re-layouts, shift_pair(): lax.slice_in_dim(cube_vals, 0, PS - 1, axis=axis_pos)  13.8 us
    unnamed x3, other arithmetic  13.3 us
  transfers between devices with their start and end apart: 5, of which 1 were waited for; matrix products, arithmetic and copies ran while one was open for 15% of the time, Pallas kernels for 0%

commit v1 on v0

--- a/solution.py
+++ b/solution.py
@@ -161,7 +161,7 @@
     partial_value = jnp.einsum("sk,sjk->jk", weights, picked, precision=highest) * (
         1.0 / math.sqrt(total_cells)
     )
-    sketch_whole = lax.psum(partial_value, ("px", "py"))
+    sketch_whole = jnp.sum(lax.all_gather(partial_value, ("px", "py")), axis=0)
     sketch_mine = lax.dynamic_slice_in_dim(sketch_whole, share_start, share_width, 1)
     normal_gram, normal_cross = normal_parts(
         sketch_whole, proj_coef, previous_coef, residual_factor

time: 612 us -> 666 us (1.088)
  other arithmetic: 81.1 us -> 112 us
  waiting for transfers between devices: 248 us -> 274 us
    all_gather x0 -> x1, waiting for transfers between devices: none -> 274 us  [body(): sketch_whole = jnp.sum(lax.all_gather(partial_value, ('px', 'py')), axis=0)]
    psum x1 -> x0, waiting for transfers between devices: 248 us -> none  [body(): sketch_whole = lax.psum(partial_value, ('px', 'py'))]
    reduce_sum x0 -> x1, other arithmetic: none -> 30.7 us  [body(): sketch_whole = jnp.sum(lax.all_gather(partial_value, ('px', 'py')), axis=0)]
  transfers between devices with their start and end apart: 5 -> 5, of which waited for: 1 -> 1; matrix products, arithmetic and copies ran while one was open for 15% -> 14% of each run, Pallas kernels for 0% -> 0%
where the time goes in v1:
time: 666 us; the launch traced here: 657 us
  waiting for transfers between devices  274 us (41%)
  local copies, waits for them, and re-layouts  138 us (21%)
  other arithmetic  112 us (17%)
  blocking collectives  80 us (12%)
  matrix products  22.9 us (3%)
  between operations  16.2 us (2%)
  starting transfers between devices  14.1 us (2%)
    all_gather x1, waiting for transfers between devices, body(): sketch_whole = jnp.sum(lax.all_gather(partial_value, ('px', 'py')), axis=0)  274 us
    psum x1, blocking collectives, body(): proj_coef = lax.psum(local_gram, ('px', 'py')) / total_cells  80 us
    sub x1, other arithmetic, apply_operator(): summed = diag_sum * centre_vals - weighted  37.8 us
    reduce_sum x1, other arithmetic, body(): sketch_whole = jnp.sum(lax.all_gather(partial_value, ('px', 'py')), axis=0)  30.7 us
    slice x2, local copies, waits for them, and re-layouts, shift_pair(): lax.slice_in_dim(cube_vals, 1, PS, axis=axis_pos)  26.7 us
    gather x1, local copies, waits for them, and re-layouts, body(): picked = jnp.take(spread, sample_rows % CELLS, axis=2)  21.6 us
    slice x4, local copies, waits for them, and re-layouts, shift_pair(): lax.slice_in_dim(cube_vals, 0, PS - 1, axis=axis_pos)  13.8 us
  transfers between devices with their start and end apart: 5, of which 1 were waited for; matrix products, arithmetic and copies ran while one was open for 14% of the time, Pallas kernels for 0%

profile of v1, /device:TPU:1, one launch (start us, length us, event | category | flops | bytes accessed | tf_op | source)
XLA Modules:
  0.0 657.1 jit_solution(306541821992453199)
XLA Ops:
  7.2 1.2 dynamic_slice.13
  8.5 0.6 compare_convert_fusion
  9.1 2.3 bitcast_multiply_fusion.2
  11.7 2.4 copy.21
  14.0 8.6 %reshape.92 = f32[6,17,16,16,16]{4,3,2,0,1:T(8,128)} reshape(f32[6,17,4096]{2,0,1:T(8,128)} %copy.21) | data formatting | bytes 3342336 | tf_op jit(solution)/shard_map/reshape | solution.py:69
  22.6 0.9 slice.167
  23.7 1.3 collective-permute-start.1
  26.3 3.2 constant_dynamic-slice_fusion.1
  29.5 3.9 copy.22
  33.3 0.9 slice.163
  34.3 5.2 collective-permute-start
  39.5 10.8 %slice_reduce_fusion = (f32[6,17,16,16]{3,2,0,1:T(8,128)}, f32[6,17,16,16]{3,2,0,1:T(8,128)}) fusion(f32[6,17,16,16,16]{4,3,2,0,1:T(8,128)} %reshape.92), kind=kLoop, calls=%fused_computation.34 | loop fusion | bytes 417792 | tf_op jit(solution)/shard_map/slice | solution.py:74
  50.2 1.5 reshape.113
  51.7 0.8 copy.47
  52.5 4.6 collective-permute-start.2
  57.1 1.5 reshape.114
  58.6 0.8 copy.48
  59.3 3.0 collective-permute-start.3
  62.4 17.5 %fusion.102 = (f32[6,16,15,16,16]{4,3,2,0,1:T(8,128)}, f32[6,16,15,16,16]{4,3,2,0,1:T(8,128)}) fusion(f32[6,17,16,16,16]{4,3,2,0,1:T(8,128)} %reshape.92), kind=kLoop, calls=%fused_computation.173 | loop fusion | bytes 5898240 | tf_op jit(solution)/shard_map/slice | solution.py:59
  79.8 1.2 slice_bitcast_fusion.1
  81.1 9.2 %fusion.101 = (f32[6,16,16,15,16]{4,3,2,0,1:T(8,128)}, f32[6,16,16,15,16]{4,3,2,0,1:T(8,128)}) fusion(f32[6,17,16,16,16]{4,3,2,0,1:T(8,128)S(1)} %bitcast.140), kind=kLoop, calls=%fused_computation.172 | loop fusion | bytes 5898240 | tf_op jit(solution)/shard_map/slice | solution.py:59
  90.3 9.8 %fusion.100 = (f32[6,16,16,16,15]{4,3,2,0,1:T(8,128)}, f32[6,16,16,16,15]{4,3,2,0,1:T(8,128)}) fusion(f32[6,17,16,16,16]{4,3,2,0,1:T(8,128)S(1)} %bitcast.140), kind=kLoop, calls=%fused_computation.171 | loop fusion | bytes 5898240 | tf_op jit(solution)/shard_map/slice | solution.py:54
  100.1 1.4 fusion.99
  101.5 1.2 fusion.97
  102.8 1.3 fusion.98
  105.3 1.4 copy.54
  106.7 1.4 copy.55
  109.1 4.0 bitcast_multiply_fusion.1
  114.3 1.3 copy.53
  115.8 0.8 reduce.7
  116.7 1.3 pad_select_fusion
  118.1 0.8 slice_bitcast_fusion.3
  118.9 3.5 fusion.30
  122.4 1.3 slice_bitcast_fusion
  123.7 0.9 copy.31
  124.6 1.2 reshape_squeeze.7
  125.8 2.1 slice.185
  127.9 1.4 slice.175
  129.3 0.9 copy.29
  130.2 1.2 reshape_squeeze.6
  131.4 2.1 slice.182
  133.5 0.8 slice.171
  134.3 5.0 add_bitcast_fusion
  139.3 37.8 %fusion = f32[6,16,16,16,16]{4,3,2,0,1:T(8,128)} fusion(f32[6,17,16,16,16]{4,3,2,0,1:T(8,128)} %reshape.92, f32[6,16,15,16,16]{4,3,2,0,1:T(8,128)} %get-tuple-element.29, f32[6,16,1,16,16]{4,3,2,0,1:T(8,128)} %get-tuple-element.41, f32[6,16,1,16,16]{4,3,2,0,1:T(8,128)} %get-tuple-element.40, f32[6,16,15,16,16]{4,3,2,0,1:T(8,128)} %get-tuple-element.28, ...), kind=kLoop, calls=%fused_computation.2 | loop fusion | flops 6684672 | bytes 13074432 | tf_op jit(solution)/shard_map/sub | solution.py:103
  177.1 10.5 %reshape.115 = f32[6,16,4096]{2,0,1:T(8,128)} reshape(f32[6,16,16,16,16]{4,3,2,0,1:T(8,128)} %fusion) | data formatting | bytes 3145728 | tf_op jit(solution)/shard_map/reshape | solution.py:104
  187.6 4.7 fusion.14
  192.3 80.0 %psum.7 = f32[32,16]{0,1:T(8,128)S(1)} all-reduce(f32[32,16]{0,1:T(8,128)S(1)} %fusion.14), channel_id=1, replica_groups=mesh['px'=32,'py'=8] {'px','py'}, use_global_device_ids=true, to_apply=%region_0.0 | all-reduce | flops 512 | bytes 4096 | tf_op jit(solution)/shard_map/psum | solution.py:155
  272.4 4.1 fusion.6
  276.8 0.9 copy-done.5
  277.6 4.0 fusion.7
  281.6 5.7 convolution_bitcast_fusion.1
  287.3 9.7 %copy.50 = f32[6,48,32,128]{1,0,3,2:T(8,128)} copy(f32[6,48,32,128]{3,2,1,0:T(8,128)} %convolution_bitcast_fusion.1) | data formatting | bytes 9437184 | tf_op jit(solution)/shard_map/reshape | solution.py:47
  297.0 21.6 %gather_fusion = f32[2048,6,48]{2,1,0:T(8,128)} fusion(f32[6,48,4096]{1,0,2:T(8,128)} %bitcast.141, s32[2048]{0:T(1024)S(1)} %copy-done.10), kind=kCustom, calls=%fused_computation | custom fusion | bytes 4726784 | tf_op jit(solution)/shard_map/jit(_take)/gather | solution.py:158
  318.6 13.2 %multiply_reduce_fusion = f32[2048,48]{1,0:T(8,128)S(1)} fusion(f32[2048,6,48]{2,1,0:T(8,128)} %gather_fusion, f32[2048,6]{1,0:T(8,128)S(1)} %copy-done.7, pred[2048]{0:T(1024)(128)(4,1)S(1)} %copy-done.15), kind=kLoop, calls=%fused_computation.12 | loop fusion | flops 1671168 | bytes 2803712
  332.2 0.8 multiply_bitcast_fusion
  333.0 274.2 %all-gather.3.cloned.1.call-done = f32[12288,2048]{1,0:T(8,128)} async-done(((f32[48,2048]{1,0:T(8,128)}), f32[12288,2048]{1,0:T(8,128)}) %all-gather.3.cloned.1.call-update) | async-done | bytes 100663312 | tf_op jit(solution)/shard_map/all_gather | solution.py:164
  607.2 30.7 %reduce_sum.9 = f32[48,2048]{1,0:T(8,128)S(1)} reduce(f32[256,48,2048]{2,1,0:T(8,128)} %bitcast.43, f32[]{:T(128)} %constant.128.clone.1), dimensions={0}, to_apply=%region_2.3 | reduce | flops 25067520 | bytes 101056512 | tf_op jit(solution)/shard_map/reduce_sum | solution.py:164
  638.2 0.7 copy.37
  638.9 1.8 fusion.27
  641.4 0.7 fusion.23
  642.1 2.9 cholesky.16
  645.7 0.7 fusion.53
  646.4 2.4 custom-call.8
  649.1 0.8 fusion.60
  (76 shorter events, 6.7 us)
Async XLA Ops:
  7.2 631.7 %copy-start = (f32[16,16]{1,0:T(8,128)S(1)}, f32[16,16]{1,0:T(8,128)}, u32[]{:S(2)}) copy-start(f32[16,16]{1,0:T(8,128)} %param.13) | copy-start | bytes 3076
  7.2 4.3 copy-start.9
  7.2 600.0 %all-gather.3.cloned.1.call-start = ((), (), s32[]{:S(2)}) async-start(), calls=%async_computation | async-start | bytes 101056512 | tf_op jit(solution)/shard_map/all_gather | solution.py:164
  9.1 104.6 %copy-start.12 = (f32[6]{0:T(128)}, f32[6]{0:T(128)S(1)}, u32[]{:S(2)}) copy-start(f32[6]{0:T(128)S(1)} %compare_convert_fusion) | copy-start | bytes 76
  23.7 92.0 %collective-permute-start.1 = (f32[1,17,256]{2,0,1:T(1,128)S(1)}, f32[1,17,256]{2,0,1:T(1,128)S(1)}, u32[]{:S(2)}, u32[]{:S(2)}) collective-permute-start(f32[1,17,256]{2,0,1:T(1,128)S(1)} %stack_reshape_squeeze.7), channel_id=1, source_target_pairs={{8,0},{16,8},{24,16},{32,24},{40,32},{48,40},{56,48},{64,56},{72,6... | collective-permute-start | bytes 52232 | tf_op jit(solution)/shard_map/ppermute | solution.py:23
  34.3 81.5 %collective-permute-start = (f32[1,17,256]{2,0,1:T(1,128)S(1)}, f32[1,17,256]{2,0,1:T(1,128)}, u32[]{:S(2)}, u32[]{:S(2)}) collective-permute-start(f32[1,17,256]{2,0,1:T(1,128)S(1)} %copy.46), channel_id=1, source_target_pairs={{0,8},{8,16},{16,24},{24,32},{32,40},{40,48},{48,56},{56,64},{64,7... | collective-permute-start | bytes 52232 | tf_op jit(solution)/shard_map/ppermute | solution.py:20
  52.5 76.8 %collective-permute-start.2 = (f32[1,6,17,256]{3,0,2,1:T(1,128)}, f32[1,6,17,256]{3,0,2,1:T(1,128)}, u32[]{:S(2)}, u32[]{:S(2)}) collective-permute-start(f32[1,6,17,256]{3,0,2,1:T(1,128)} %copy.47), channel_id=1, source_target_pairs={{0,1},{1,2},{2,3},{3,4},{4,5},{5,6},{6,7},{8,9},{9,10},{10,11},{11... | collective-permute-start | bytes 313352 | tf_op jit(solution)/shard_map/ppermute | solution.py:20
  58.6 21.2 %slice-start = ((s8[13369344]{0:T(1024)(128)(4,1)}), s8[4194304]{0:T(1024)(128)(4,1)S(1)}, s32[]{:S(2)}) async-start(s8[13369344]{0:T(1024)(128)(4,1)} %bitcast.139), calls=%async_computation.1 | async-start | bytes 8388608
  59.3 20.5 %slice-start.1 = ((s8[13369344]{0:T(1024)(128)(4,1)}), s8[4194304]{0:T(1024)(128)(4,1)S(1)}, s32[]{:S(2)}) async-start(s8[13369344]{0:T(1024)(128)(4,1)} %bitcast.139), calls=%async_computation.2 | async-start | bytes 8388608
  59.3 20.5 %slice-start.2 = ((s8[13369344]{0:T(1024)(128)(4,1)}), s8[4194304]{0:T(1024)(128)(4,1)S(1)}, s32[]{:S(2)}) async-start(s8[13369344]{0:T(1024)(128)(4,1)} %bitcast.139), calls=%async_computation.3 | async-start | bytes 8388608
  59.3 20.5 %slice-start.3 = ((s8[13369344]{0:T(1024)(128)(4,1)}), s8[786432]{0:T(1024)(128)(4,1)S(1)}, s32[]{:S(2)}) async-start(s8[13369344]{0:T(1024)(128)(4,1)} %bitcast.139), calls=%async_computation.4 | async-start | bytes 1572864
  59.3 64.3 %collective-permute-start.3 = (f32[1,6,17,256]{3,0,2,1:T(1,128)}, f32[1,6,17,256]{3,0,2,1:T(1,128)}, u32[]{:S(2)}, u32[]{:S(2)}) collective-permute-start(f32[1,6,17,256]{3,0,2,1:T(1,128)} %copy.48), channel_id=1, source_target_pairs={{1,0},{2,1},{3,2},{4,3},{5,4},{6,5},{7,6},{9,8},{10,9},{11,10},{12... | collective-permute-start | bytes 313352 | tf_op jit(solution)/shard_map/ppermute | solution.py:23
  100.1 3.9 copy-start.11
  100.1 5.1 copy-start.3
  101.5 5.2 copy-start.4
  102.8 5.4 copy-start.8
  102.8 5.5 copy-start.16
  116.7 5.6 copy-start.6
  177.1 10.5 %copy-start.13 = (f32[6]{0:T(128)S(1)}, f32[6]{0:T(128)}, u32[]{:S(2)}) copy-start(f32[6]{0:T(128)} %copy-done.12) | copy-start | bytes 76
  272.3 5.3 copy-start.1
  272.3 5.3 copy-start.2
  276.5 1.1 copy-start.5
  287.3 9.7 %copy-start.10 = (s32[2048]{0:T(1024)S(1)}, s32[2048]{0:T(1024)}, u32[]{:S(2)}) copy-start(s32[2048]{0:T(1024)} %get-tuple-element.33) | copy-start | bytes 24580
  297.0 21.6 %copy-start.7 = (f32[2048,6]{1,0:T(8,128)S(1)}, f32[2048,6]{1,0:T(8,128)}, u32[]{:S(2)}) copy-start(f32[2048,6]{1,0:T(8,128)} %copy.53) | copy-start | bytes 147460
  297.0 21.6 %copy-start.15 = (pred[2048]{0:T(1024)(128)(4,1)S(1)}, pred[2048]{0:T(1024)(128)(4,1)}, u32[]{:S(2)}) copy-start(pred[2048]{0:T(1024)(128)(4,1)} %compare_and_fusion) | copy-start | bytes 6148
  607.2 33.5 %copy-start.14 = (f32[32,16]{0,1:T(8,128)S(1)}, f32[32,16]{0,1:T(8,128)}, u32[]{:S(2)}) copy-start(f32[32,16]{0,1:T(8,128)} %param.14) | copy-start | bytes 6148
Sparse Core Ops, SparseCore 0:
  333.1 274.0 all-gather.2
